TPU v7x, 32 devices: a whole 2x2x4 slice. The times are simulated.
32 devices in a mesh: groups: 2 (over x), wide: 16 (over z, y, core).
Axes of the slice: x: 2, y: 2, z: 4, core: 2. Of those that a mesh axis runs over, the one named last changes fastest.
Arguments:
- iterate: float32 [8192, 128], P(('groups', 'wide')), parts along dimension 0, may hold values from -6 to 6
- rhs: float32 [8192, 128], P(('groups', 'wide')), parts along dimension 0, may hold values from -6 to 6
- schur: float32 [32, 384, 384], P(('groups', 'wide')), parts along dimension 0
- near_block: float32 [8192, 256], P(('groups', 'wide')), parts along dimension 0
- u_basis: float32 [32, 32, 4096], P('groups', None, 'wide'), parts along dimension 0, may hold values from -0.375 to 0.375
- v_basis: float32 [32, 32, 4096], P('groups', None, 'wide'), parts along dimension 0, may hold values from -0.375 to 0.375
- tile_rank: int32 [32, 16], P('groups', 'wide'), parts along dimension 0, may hold values from 1 to 32
- send_rows: int32 [32, 3, 128], P(('groups', 'wide')), parts along dimension 0, may hold values from 0 to 255
- send_count: int32 [32, 3], P(('groups', 'wide')), parts along dimension 0, may hold values from 0 to 128, as said below
- precond: float32 [8192], P(('groups', 'wide')), parts along dimension 0, may hold values from 0.1 to 1
Outputs:
- updated: float32 [8192, 128], P(('groups', 'wide')), parts along dimension 0
- residual: float32 [8192, 128], P(('groups', 'wide')), parts along dimension 0
There are 2 independent parts, one for each index of `groups`. A program takes and returns all parts, laid end to end along the dimension named above; each array names one. Nothing has to cross between parts.
Inputs may be any that keep to these rules, and one draw needn't show every extreme that they name: send_count[p, 0] is 0 for p = 0 and send_count[p, 2] is 0 for p = 15; a block is full in every draw.
All inputs are finite; a program needn't handle non-finite values.
Results may differ from a plain program's by a relative error of at most 0.0003.
Values sent between devices are 32-bit elements; how exact they have to be, the bound alone decides.
A program may use at most 64 MiB of HBM per device.

v0:
```python
import functools
import math

import jax
import jax.numpy as jnp
from jax import lax
from jax.experimental import pallas as pl
from jax.experimental.pallas import tpu as pltpu
from jax.sharding import PartitionSpec as P

EARLY = 2
STRIDE = False
FIRST = 0
JOIN = 0
TAIL = 1
MESH = pl.DeviceIdType.MESH
F32 = jnp.float32
BF16 = jnp.bfloat16


def halves(x):
    high = x.astype(BF16)
    low = (x - high.astype(F32)).astype(BF16)
    return high, low


def mm(a, b):
    return jnp.dot(a, b, preferred_element_type=F32)


def pair(x):
    high, low = halves(x)
    return jnp.concatenate([high, low], axis=1), high


def fold(p):
    width = p.shape[1] // 2
    return p[:, :width] + p[:, width:]


def product(a_high, a_low, b_both, b_high):
    return fold(mm(a_high, b_both)) + mm(a_low, b_high)


def kernel(
    n,
    iterate_hbm, schur_hbm, near_hbm, u_hbm, v_hbm, rank_hbm, rows_hbm, count_hbm,
    out_ref,
    iterate, schur, near, u, v, rank, rows, count,
    out_face, in_face, out_force, in_force, sent, gathered,
    u_high, u_low, s_high, s_low,
    load_sem, face_send, face_recv, force_send, force_recv, send_sem, recv_sem,
):
    me = lax.axis_index("wide")
    loads = iterate.shape[1]
    face = rows.shape[2]
    rank_top = v.shape[1]
    rows_here = iterate.shape[0]
    power = n & (n - 1) == 0
    bits = [1 << b for b in range(n.bit_length()) if 1 << b < n]
    flips = [bit * (1 - 2 * lax.rem(lax.div(me, bit), 2)) for bit in bits]

    def to_of(k):
        if power:
            return me + sum(flip for bit, flip in zip(bits, flips) if k & bit)
        return lax.rem(me + k, n)

    def from_of(k):
        return to_of(k) if power else lax.rem(me - k + n, n)

    barrier = pltpu.get_barrier_semaphore()
    for k in range(n - 1, 0, -1):
        pl.semaphore_signal(barrier, inc=1, device_id={"wide": to_of(k)}, device_id_type=MESH)

    group = math.gcd(n, max(1, 128 // rank_top))
    if STRIDE:
        groups = [[step + n // group * g for g in range(group - 1, -1, -1)] for step in range(n // group - 1, -1, -1)]
    else:
        halfway = n // 2 // group * group
        firsts = [*range(halfway, n - group + 1, group), *range(halfway - group, -1, -group)]
        groups = [[first + g for g in range(group)] for first in firsts]
    slot_of = {k: at for at, k in enumerate(k for members in groups for k in members)}

    names = {}
    def load(name, at, source, target):
        names[name] = pltpu.make_async_copy(source, target, load_sem.at[at])
        names[name].start()

    load("iterate", 0, iterate_hbm, iterate)
    load("rank", 1, rank_hbm, rank)
    for at, k in enumerate(slot_of):
        if at < group:
            load(k, 7 + at, v_hbm.at[to_of(k)], v.at[at])
    load("rows", 2, rows_hbm, rows)
    load("count", 3, count_hbm, count)
    for at, k in enumerate(slot_of):
        if at >= group:
            load(k, 7 + at, v_hbm.at[to_of(k)], v.at[at])
    load("schur", 4, schur_hbm, schur)
    load("u", 5, u_hbm, u)
    load("near", 6, near_hbm, near)

    @pl.when(me == 0)
    def _():
        in_face[2] = jnp.zeros_like(in_face[2])
        in_force[0] = jnp.zeros_like(in_force[0])

    @pl.when(me == n - 1)
    def _():
        in_face[0] = jnp.zeros_like(in_face[0])
        in_force[2] = jnp.zeros_like(in_force[2])

    names["iterate"].wait()
    it_both, it_high = pair(iterate[...])
    rank_ids = lax.broadcasted_iota(jnp.int32, (rank_top, loads), 0)
    copies = {
        k: pltpu.make_async_remote_copy(
            src_ref=sent.at[slot], dst_ref=gathered.at[slot], send_sem=send_sem.at[slot],
            recv_sem=recv_sem.at[slot], device_id={"wide": to_of(k)}, device_id_type=MESH,
        )
        for k, slot in slot_of.items() if k > 0
    }

    def compress(members):
        for k in members:
            names[k].wait()
        block = jnp.concatenate([v[slot_of[k]] for k in members], axis=0)
        v_high, v_low = halves(block)
        coeff = product(v_high, v_low, it_both, it_high)
        for g, k in enumerate(members):
            part = coeff[g * rank_top : (g + 1) * rank_top]
            part = jnp.where(rank_ids < rank[0, to_of(k)], part, 0.0)
            if k == 0:
                gathered[slot_of[k]] = part
            else:
                sent[slot_of[k]] = part

    def send(members):
        for k in members:
            if k > 0:
                copies[k].start()

    names["rank"].wait()
    early = min(EARLY, len(groups))
    for members in groups[:early]:
        compress(members)

    if FIRST:
        pl.semaphore_wait(barrier, n - 1)
        for members in groups[:early]:
            send(members)

    names["rows"].wait()
    names["count"].wait()
    slot_ids = lax.broadcasted_iota(jnp.int32, (1, face), 1)
    row_of = []
    for o in range(3):
        row_of.append(jnp.where(slot_ids < count[0, o], rows[o], -1))
    lanes = lax.broadcasted_iota(jnp.int32, (face, rows_here), 1)
    for o in (0, 2, 1):
        column = jnp.broadcast_to(row_of[o].astype(F32), (face, face)).T[:, :1].astype(jnp.int32)
        select = (column == lanes).astype(F32).astype(BF16)
        picked = fold(mm(select, it_both))
        if o == 1:
            in_face[1] = picked
        else:
            out_face[o // 2] = picked

    if not FIRST:
        pl.semaphore_wait(barrier, n - 1)

    def face_copy(o, source, target, send, recv, peer):
        return pltpu.make_async_remote_copy(
            src_ref=source, dst_ref=target, send_sem=send.at[o // 2], recv_sem=recv.at[o // 2],
            device_id={"wide": peer}, device_id_type=MESH,
        )

    below, above = lax.rem(me + n - 1, n), lax.rem(me + 1, n)
    faces = {
        0: face_copy(0, out_face.at[0], in_face.at[0], face_send, face_recv, below),
        2: face_copy(2, out_face.at[1], in_face.at[2], face_send, face_recv, above),
    }
    returns = {
        0: face_copy(0, out_force.at[0], in_force.at[0], force_send, force_recv, above),
        2: face_copy(2, out_force.at[1], in_force.at[2], force_send, force_recv, below),
    }
    has_below, has_above = me > 0, me < n - 1

    @pl.when(has_below)
    def _():
        faces[0].start()

    @pl.when(has_above)
    def _():
        faces[2].start()

    if not FIRST:
        for members in groups[:early]:
            send(members)
    for members in groups[early:]:
        compress(members)
        send(members)

    names["schur"].wait()
    high, low = halves(schur[0])
    s_high[...] = high
    s_low[...] = low
    mid = slice(face, 2 * face)
    b_both, b_high = pair(in_face[1])
    force = product(s_high[:, mid], s_low[:, mid], b_both, b_high)
    @pl.when(has_above)
    def _():
        faces[0].wait_recv()

    @pl.when(has_below)
    def _():
        faces[2].wait_recv()

    for o in (0, 2):
        span = slice(o * face, (o + 1) * face)
        b_both, b_high = pair(in_face[o])
        force = force + product(s_high[:, span], s_low[:, span], b_both, b_high)
    out_force[0] = force[:face]
    out_force[1] = force[2 * face :]
    in_force[1] = force[mid]

    @pl.when(has_above)
    def _():
        returns[0].start()

    @pl.when(has_below)
    def _():
        returns[2].start()

    names["u"].wait()
    names["near"].wait()
    for at, members in enumerate(groups):
        block = jnp.concatenate([u[from_of(k)] for k in members], axis=0).T
        high, low = halves(block)
        span = slice(at * group * rank_top, (at + 1) * group * rank_top)
        u_high[:, span] = high
        u_low[:, span] = low
    near_high, near_low = halves(near[...])
    out_ref[...] = product(near_high, near_low, it_both, it_high)

    def far(first, size):
        for k, slot in slot_of.items():
            if k > 0 and first <= slot < first + size:
                copies[k].wait_recv()
        got = gathered[first : first + size].reshape(size * rank_top, loads)
        b_both, b_high = pair(got)
        span = slice(first * rank_top, (first + size) * rank_top)
        return product(u_high[:, span], u_low[:, span], b_both, b_high)

    spans = [(at * group, group) for at in range(len(groups))]
    half = len(spans) // 2
    spans = spans[half:][::-1] + spans[:half]
    if JOIN and half > 1:
        spans = spans[:-half] + [(at * group, 2 * group) for at in range(0, half - 1, 2)]
        if half % 2:
            spans = spans[:-1] + [((half - 1) * group, group), spans[-1]]
    for first, size in spans[: len(spans) - TAIL]:
        out_ref[...] += far(first, size)

    @pl.when(has_below)
    def _():
        returns[0].wait_recv()

    @pl.when(has_above)
    def _():
        returns[2].wait_recv()

    total = out_ref[...]
    place = lax.broadcasted_iota(jnp.int32, (rows_here, face), 0)
    for o in range(3):
        scatter = (place == row_of[o]).astype(F32).astype(BF16)
        b_both, _ = pair(in_force[o])
        total = total + fold(mm(scatter, b_both))
    for first, size in spans[len(spans) - TAIL :]:
        total = total + far(first, size)
    out_ref[...] = total

    @pl.when(has_below)
    def _():
        faces[0].wait_send()
        returns[2].wait_send()

    @pl.when(has_above)
    def _():
        faces[2].wait_send()
        returns[0].wait_send()

    for k in range(1, n):
        copies[k].wait_send()


def body(
    iterate, rhs, schur, near_block, u_basis, v_basis, tile_rank, send_rows, send_count, precond
):
    n = lax.axis_size("wide")
    rows_here, loads = iterate.shape
    face = send_rows.shape[2]
    tiles, rank_top, _ = u_basis.shape
    tile_rank = tile_rank.reshape(1, tiles)
    send_rows = send_rows.reshape(3, 1, face)
    dma = pltpu.SemaphoreType.DMA
    applied = pl.pallas_call(
        functools.partial(kernel, n),
        out_shape=pltpu.VMEM((rows_here, loads), F32),
        in_specs=[pl.BlockSpec(memory_space=pl.ANY)] * 8,
        out_specs=pl.BlockSpec(memory_space=pltpu.VMEM),
        scratch_shapes=[
            pltpu.VMEM(iterate.shape, F32),
            pltpu.VMEM(schur.shape, F32),
            pltpu.VMEM(near_block.shape, F32),
            pltpu.VMEM(u_basis.shape, F32),
            pltpu.VMEM(v_basis.shape, F32),
            pltpu.SMEM(tile_rank.shape, jnp.int32),
            pltpu.VMEM(send_rows.shape, jnp.int32),
            pltpu.SMEM(send_count.shape, jnp.int32),
            pltpu.VMEM((2, face, loads), F32),
            pltpu.VMEM((3, face, loads), F32),
            pltpu.VMEM((2, face, loads), F32),
            pltpu.VMEM((3, face, loads), F32),
            pltpu.VMEM((n, rank_top, loads), F32),
            pltpu.VMEM((n, rank_top, loads), F32),
            pltpu.VMEM((rows_here, tiles * rank_top), BF16),
            pltpu.VMEM((rows_here, tiles * rank_top), BF16),
            pltpu.VMEM(schur.shape[1:], BF16),
            pltpu.VMEM(schur.shape[1:], BF16),
            dma((7 + n,)),
            dma((2,)),
            dma((2,)),
            dma((2,)),
            dma((2,)),
            dma((n,)),
            dma((n,)),
        ],
        compiler_params=pltpu.CompilerParams(collective_id=0, has_side_effects=True),
    )(iterate, schur, near_block, u_basis, v_basis, tile_rank, send_rows, send_count)
    residual = rhs - applied
    updated = iterate + precond[:, None] * residual
    return (updated, residual)


def solution(mesh):
    in_specs = (
        P(("groups", "wide"), None),
        P(("groups", "wide"), None),
        P(("groups", "wide"), None, None),
        P(("groups", "wide"), None),
        P("groups", None, "wide"),
        P("groups", None, "wide"),
        P("groups", "wide"),
        P(("groups", "wide"), None, None),
        P(("groups", "wide"), None),
        P(("groups", "wide")),
    )
    out_specs = (P(("groups", "wide"), None), P(("groups", "wide"), None))
    return jax.shard_map(body, mesh=mesh, in_specs=in_specs, out_specs=out_specs, check_vma=False)
```

profile of v0, /device:TPU:16, one launch (start us, length us, event | category | flops | bytes accessed | tf_op | source)
XLA Modules:
  0.0 15.5 jit_solution(7687620342803679169)
XLA Ops:
  0.6 0.0 copy-start
  0.6 0.0 copy-start.1
  0.7 0.0 copy-start.2
  0.7 14.0 %shard_map.113 = f32[256,128]{1,0:T(8,128)S(1)} custom-call(f32[256,128]{1,0:T(8,128)} %iterate_hbm.1, f32[1,384,384]{2,1,0:T(8,128)} %schur_hbm.1, f32[256,256]{1,0:T(8,128)} %near_hbm.1, f32[16,32,256]{2,1,0:T(8,128)} %u_hbm.1, f32[16,32,256]{2,1,0:T(8,128)} %v_hbm.1, s32[1,16]{1,0:T(1,128)} %bitcast.3, s32[3,1,128]{2,1,0:T(1,128)} %bitcast.2, ...), custom_call_target="tpu_custom_call" | custom-call | tf_op jit(solution)/shard_map/pallas_call | solution.py:307
  14.7 0.0 copy-done
  14.7 0.0 copy-done.1
  14.7 0.0 copy-done.2
  14.7 0.8 %multiply_add_fusion = (f32[256,128]{1,0:T(8,128)}, f32[256,128]{1,0:T(8,128)}) fusion(f32[256,128]{1,0:T(8,128)S(1)} %copy-done, f32[256]{0:T(256)S(1)} %copy-done.2, f32[256,128]{1,0:T(8,128)S(1)} %copy-done.1, f32[256,128]{1,0:T(8,128)S(1)} %shard_map.113), kind=kLoop, calls=%fused_computation | loop fusion | flops 98304 | bytes 656384 | tf_op jit(solution)/shard_map/add | solution.py:342
Async XLA Ops:
  0.6 14.0 %copy-start = (f32[256,128]{1,0:T(8,128)S(1)}, f32[256,128]{1,0:T(8,128)}, u32[]{:S(2)}) copy-start(f32[256,128]{1,0:T(8,128)} %iterate_hbm.1) | copy-start | bytes 393220
  0.6 14.0 %copy-start.1 = (f32[256,128]{1,0:T(8,128)S(1)}, f32[256,128]{1,0:T(8,128)}, u32[]{:S(2)}) copy-start(f32[256,128]{1,0:T(8,128)} %param.11) | copy-start | bytes 393220
  0.7 14.0 %copy-start.2 = (f32[256]{0:T(256)S(1)}, f32[256]{0:T(256)}, u32[]{:S(2)}) copy-start(f32[256]{0:T(256)} %param.19) | copy-start | bytes 3076
where the time goes:
time: 15.6 us; the launch traced here: 15.5 us
  Pallas kernels  14 us (90%)
  other arithmetic  0.76 us (5%)
  between operations  0.69 us (4%)
    pallas_call x1, Pallas kernels, body(): pl.pallas_call(functools.partial(kernel, n), out_shape=pltpu.VMEM((rows_h...  14 us
    add x1, other arithmetic, body(): updated = iterate + precond[:, None] * residual  0.76 us

commit v1 on v0

v1 whole, which is shorter than its diff:
```python
import functools
import math

import jax
import jax.numpy as jnp
from jax import lax
from jax.experimental import pallas as pl
from jax.experimental.pallas import tpu as pltpu
from jax.sharding import PartitionSpec as P

MESH = pl.DeviceIdType.MESH
F32 = jnp.float32
BF16 = jnp.bfloat16


def halves(x):
    high = x.astype(BF16)
    low = (x - high.astype(F32)).astype(BF16)
    return high, low


def mm(a, b):
    return jnp.dot(a, b, preferred_element_type=F32)


def pair(x):
    high, low = halves(x)
    return jnp.concatenate([high, low], axis=1), high


def fold(p):
    width = p.shape[1] // 2
    return p[:, :width] + p[:, width:]


def product(a_high, a_low, b_both, b_high):
    return fold(mm(a_high, b_both)) + mm(a_low, b_high)


def kernel(
    n,
    iterate_hbm, schur_hbm, near_hbm, u_hbm, v_hbm, rank_hbm, rows_hbm, count_hbm,
    out_ref,
    iterate, schur, near, u, v, rank, rows, count,
    edge_out, in_face, in_force, sent, gathered, u_high, u_low,
    load_sem, edge_send, face_recv, force_recv, send_sem, recv_sem, late_sem,
):
    me = lax.axis_index("wide")
    loads = iterate.shape[1]
    face = rows.shape[2]
    rank_top = v.shape[1]
    rows_here = iterate.shape[0]

    blocks = 4 if n % 4 == 0 else 1
    per_block = n // blocks
    group = math.gcd(per_block, max(1, 128 // rank_top))
    chunks = per_block // group
    block = lax.div(me, per_block)
    mine = lax.div(me, group)
    place_in_block = lax.rem(me, per_block)
    place_in_group = lax.rem(me, group)

    def by_block(first, second, third, fourth):
        at_least = [lax.div(block + 2, 3), lax.div(block, 2), lax.div(block, 3)]
        return first + (second - first) * at_least[0] + (third - second) * at_least[1] + (fourth - third) * at_least[2]

    if blocks == 4:
        send_order = [by_block(1, 2, 0, 0), by_block(0, 0, 1, 1), by_block(2, 1, 2, 2), 3]
        own_slot = by_block(1, 2, 2, 3)
        recv_order = [block, by_block(1, 0, 1, 2), by_block(2, 2, 0, 1), by_block(3, 3, 3, 0)]
    else:
        send_order, own_slot, recv_order = [0], 0, [0]

    def load(at, source, target):
        copy = pltpu.make_async_copy(source, target, load_sem.at[at])
        copy.start()
        return copy

    def load_v(slot, c):
        first = send_order[slot] * per_block + c * group
        at = slot * chunks + c
        return load(7 + at, v_hbm.at[pl.ds(first, group)], v.at[pl.ds(at * group, group)])

    iterate_load = load(0, iterate_hbm, iterate)
    barrier = pltpu.get_barrier_semaphore()

    def tell(semaphore, target):
        pl.semaphore_signal(semaphore, inc=1, device_id={"wide": target}, device_id_type=MESH)

    def tell_block(semaphore, target_block):
        for k in range(per_block):
            tell(semaphore, target_block * per_block + lax.rem(place_in_block + k, per_block))

    for k in range(1, per_block):
        tell(barrier, block * per_block + lax.rem(place_in_block + k, per_block))
    if blocks == 4:
        for target in range(blocks):
            last = [1, 2, 2, 3][target]

            @pl.when(jnp.logical_and(block != target, block <= last))
            def _():
                tell_block(barrier, target)

    def enter():
        pl.semaphore_wait(barrier, (per_block * by_block(2, 3, 3, 4) if blocks == 4 else n) - 1)

    def announce():
        if blocks == 4:
            @pl.when(block == 2)
            def _():
                tell_block(late_sem.at[0], 0)

            @pl.when(block == 3)
            def _():
                for target in range(3):
                    tell_block(late_sem.at[1], target)

    def late(which):
        if blocks == 4:
            @pl.when(block == 0 if which == 0 else block < 3)
            def _():
                pl.semaphore_wait(late_sem.at[which], per_block)

    rows_load = load(2, rows_hbm, rows)
    count_load = load(3, count_hbm, count)
    rank_load = load(1, rank_hbm, rank)
    v_loads = {(slot, c): load_v(slot, c) for slot in range(blocks) for c in range(chunks)}
    near_load = load(6, near_hbm, near)
    u_load = load(5, u_hbm, u)
    schur_load = load(4, schur_hbm, schur)

    @pl.when(me == 0)
    def _():
        in_face[2] = jnp.zeros_like(in_face[2])
        in_force[0] = jnp.zeros_like(in_force[0])

    @pl.when(me == n - 1)
    def _():
        in_face[0] = jnp.zeros_like(in_face[0])
        in_force[2] = jnp.zeros_like(in_force[2])

    below, above = lax.rem(me + n - 1, n), lax.rem(me + 1, n)
    has_below, has_above = me > 0, me < n - 1

    def edge_copy(side, kind, target, recv):
        return pltpu.make_async_remote_copy(
            src_ref=edge_out.at[side, kind], dst_ref=target, send_sem=edge_send.at[side], recv_sem=recv,
            device_id={"wide": above if side else below}, device_id_type=MESH,
        )

    face_down = edge_copy(0, 0, in_face.at[0], face_recv.at[0])
    face_up = edge_copy(1, 0, in_face.at[2], face_recv.at[1])
    force_up = edge_copy(1, 1, in_force.at[0], force_recv.at[0])
    force_down = edge_copy(0, 1, in_force.at[2], force_recv.at[1])

    iterate_load.wait()
    it_both, it_high = pair(iterate[...])
    rows_load.wait()
    count_load.wait()
    slot_ids = lax.broadcasted_iota(jnp.int32, (1, face), 1)
    row_of = [jnp.where(slot_ids < count[0, o], rows[o], -1) for o in range(3)]
    lanes = lax.broadcasted_iota(jnp.int32, (face, rows_here), 1)

    def picked(o):
        column = jnp.broadcast_to(row_of[o].astype(F32), (face, face)).T[:, :1].astype(jnp.int32)
        select = (column == lanes).astype(F32).astype(BF16)
        return fold(mm(select, it_both))

    edge_out[0, 0] = picked(0)
    edge_out[1, 0] = picked(2)

    rank_ids = lax.broadcasted_iota(jnp.int32, (rank_top, loads), 0)

    def compress(slot, c):
        v_loads[slot, c].wait()
        at = (slot * chunks + c) * group
        first = send_order[slot] * per_block + c * group
        v_high, v_low = halves(v[at : at + group].reshape(group * rank_top, rows_here))
        coeff = product(v_high, v_low, it_both, it_high)
        for g in range(group):
            part = coeff[g * rank_top : (g + 1) * rank_top]
            sent[at + g] = jnp.where(rank_ids < rank[0, first + g], part, 0.0)

    paired = group & (group - 1) == 0 and group > 1
    if paired:
        offsets = [int(bin(group + k)[:2:-1], 2) for k in range(group)]
        flip = lax.rem(me, 2) * (group // 2)

    def member(k):
        if not paired:
            return lax.rem(place_in_group + k, group)
        moved = place_in_group
        for bit in [1 << b for b in range(group.bit_length() - 1)]:
            on = 1 if offsets[k] & bit else 0
            change = on + lax.rem(me, 2) - 2 * on * lax.rem(me, 2) if bit == group // 2 else on
            moved = moved + change * bit * (1 - 2 * lax.rem(lax.div(place_in_group, bit), 2))
        return moved

    def send(slot, c):
        first = send_order[slot] * per_block + c * group
        for k in range(group):
            in_group = member(k)

            def start():
                pltpu.make_async_remote_copy(
                    src_ref=sent.at[(slot * chunks + c) * group + in_group], dst_ref=gathered.at[me],
                    send_sem=send_sem.at[0], recv_sem=recv_sem.at[mine],
                    device_id={"wide": first + in_group}, device_id_type=MESH,
                ).start()

            if blocks == 4 and (slot == 0 or paired and offsets[k] not in (0, group // 2)):
                start()
            else:
                pl.when(first + in_group != me)(start)

    rank_load.wait()
    steps = [(slot, c) for slot in range(blocks) for c in range(chunks)]

    def of_slot(slot):
        return [(slot, c) for c in range(chunks)]

    compress(*steps[0])
    enter()
    announce()
    waits_above = me == 3 * per_block - 1 if blocks == 4 else me < 0

    @pl.when(has_below)
    def _():
        face_down.start()

    @pl.when(jnp.logical_and(has_above, jnp.logical_not(waits_above)))
    def _():
        face_up.start()

    send(*steps[0])
    for step in steps[1 : 2 * chunks]:
        compress(*step)
        send(*step)
    for step in steps[2 * chunks :]:
        compress(*step)
    gathered[me] = sent[own_slot * per_block + place_in_block]
    if blocks == 4:
        late(0)
        for step in of_slot(2):
            send(*step)

    in_face[1] = picked(1)
    near_load.wait()
    near_high, near_low = halves(near[...])
    out_ref[...] = product(near_high, near_low, it_both, it_high)
    u_load.wait()
    for at in range(n // group):
        high, low = halves(u[at * group : (at + 1) * group].reshape(group * rank_top, rows_here).T)
        u_high[at] = high
        u_low[at] = low

    schur_load.wait()
    s_high, s_low = halves(schur[0])

    def force_part(o):
        span = slice(o * face, (o + 1) * face)
        b_both, b_high = pair(in_face[o])
        return product(s_high[:, span], s_low[:, span], b_both, b_high)

    force = force_part(1)
    if blocks == 4:
        late(1)

        @pl.when(waits_above)
        def _():
            face_up.start()

        for step in of_slot(3):
            send(*step)

    def face_wait():
        @pl.when(has_above)
        def _():
            face_down.wait_recv()

        @pl.when(has_below)
        def _():
            face_up.wait_recv()

    face_wait()
    force = force + force_part(0) + force_part(2)
    edge_out[0, 1] = force[2 * face :]
    edge_out[1, 1] = force[:face]
    in_force[1] = force[face : 2 * face]

    @pl.when(has_above)
    def _():
        force_up.start()

    @pl.when(has_below)
    def _():
        force_down.start()

    place = lax.broadcasted_iota(jnp.int32, (rows_here, face), 0)

    def scattered(o):
        scatter = (place == row_of[o]).astype(F32).astype(BF16)
        b_both, _ = pair(in_force[o])
        return fold(mm(scatter, b_both))

    def far(slot, c):
        at = recv_order[slot] * chunks + c

        def arrived(tiles):
            span = gathered.at[pl.ds(0, tiles)]
            pltpu.make_async_remote_copy(
                src_ref=span, dst_ref=span, send_sem=send_sem.at[0], recv_sem=recv_sem.at[at],
                device_id={"wide": above}, device_id_type=MESH,
            ).wait_recv()

        def wait():
            if slot > 0:
                arrived(group)
                return
            if group > 1:
                @pl.when(at == mine)
                def _():
                    arrived(group - 1)

            if chunks > 1:
                @pl.when(at != mine)
                def _():
                    arrived(group)

        wait()
        got = gathered[pl.ds(at * group, group)].reshape(group * rank_top, loads)
        b_both, b_high = pair(got)
        return product(u_high[at], u_low[at], b_both, b_high)

    out_ref[...] += scattered(1)
    order = [(slot, c) for slot in range(blocks) for c in range(chunks)]
    for slot, c in order[:-1]:
        out_ref[...] += far(slot, c)

    def force_wait():
        @pl.when(has_below)
        def _():
            force_up.wait_recv()

        @pl.when(has_above)
        def _():
            force_down.wait_recv()

    force_wait()
    out_ref[...] += scattered(0) + scattered(2)
    out_ref[...] += far(*order[-1])

    def sent_wait():
        @pl.when(has_below)
        def _():
            pltpu.make_async_remote_copy(
                src_ref=edge_out.at[0], dst_ref=edge_out.at[0], send_sem=edge_send.at[0],
                recv_sem=face_recv.at[0], device_id={"wide": below}, device_id_type=MESH,
            ).wait_send()

        @pl.when(has_above)
        def _():
            pltpu.make_async_remote_copy(
                src_ref=edge_out.at[1], dst_ref=edge_out.at[1], send_sem=edge_send.at[1],
                recv_sem=face_recv.at[1], device_id={"wide": above}, device_id_type=MESH,
            ).wait_send()

        all_sent = sent.at[pl.ds(0, n - 1)]
        pltpu.make_async_remote_copy(
            src_ref=all_sent, dst_ref=all_sent, send_sem=send_sem.at[0], recv_sem=recv_sem.at[0],
            device_id={"wide": above}, device_id_type=MESH,
        ).wait_send()

    sent_wait()


def body(
    iterate, rhs, schur, near_block, u_basis, v_basis, tile_rank, send_rows, send_count, precond
):
    n = lax.axis_size("wide")
    rows_here, loads = iterate.shape
    face = send_rows.shape[2]
    tiles, rank_top, _ = u_basis.shape
    group = math.gcd(n // 4 if n % 4 == 0 else n, max(1, 128 // rank_top))
    tile_rank = tile_rank.reshape(1, tiles)
    send_rows = send_rows.reshape(3, 1, face)
    dma = pltpu.SemaphoreType.DMA
    applied = pl.pallas_call(
        functools.partial(kernel, n),
        out_shape=pltpu.VMEM((rows_here, loads), F32),
        in_specs=[pl.BlockSpec(memory_space=pl.ANY)] * 8,
        out_specs=pl.BlockSpec(memory_space=pltpu.VMEM),
        scratch_shapes=[
            pltpu.VMEM(iterate.shape, F32),
            pltpu.VMEM(schur.shape, F32),
            pltpu.VMEM(near_block.shape, F32),
            pltpu.VMEM(u_basis.shape, F32),
            pltpu.VMEM(v_basis.shape, F32),
            pltpu.SMEM(tile_rank.shape, jnp.int32),
            pltpu.VMEM(send_rows.shape, jnp.int32),
            pltpu.SMEM(send_count.shape, jnp.int32),
            pltpu.VMEM((2, 2, face, loads), F32),
            pltpu.VMEM((3, face, loads), F32),
            pltpu.VMEM((3, face, loads), F32),
            pltpu.VMEM((n, rank_top, loads), F32),
            pltpu.VMEM((n, rank_top, loads), F32),
            pltpu.VMEM((n // group, rows_here, group * rank_top), BF16),
            pltpu.VMEM((n // group, rows_here, group * rank_top), BF16),
            dma((7 + n // group,)),
            dma((2,)),
            dma((2,)),
            dma((2,)),
            dma((1,)),
            dma((n // group,)),
            pltpu.SemaphoreType.REGULAR((2,)),
        ],
        compiler_params=pltpu.CompilerParams(collective_id=0, has_side_effects=True),
    )(iterate, schur, near_block, u_basis, v_basis, tile_rank, send_rows, send_count)
    residual = rhs - applied
    updated = iterate + precond[:, None] * residual
    return (updated, residual)


def solution(mesh):
    in_specs = (
        P(("groups", "wide"), None),
        P(("groups", "wide"), None),
        P(("groups", "wide"), None, None),
        P(("groups", "wide"), None),
        P("groups", None, "wide"),
        P("groups", None, "wide"),
        P("groups", "wide"),
        P(("groups", "wide"), None, None),
        P(("groups", "wide"), None),
        P(("groups", "wide")),
    )
    out_specs = (P(("groups", "wide"), None), P(("groups", "wide"), None))
    return jax.shard_map(body, mesh=mesh, in_specs=in_specs, out_specs=out_specs, check_vma=False)
```

time: 15.6 us -> 14 us (0.90)
  the two profiles are of different devices: /device:TPU:16 before, /device:TPU:1 now
where the time goes in v1:
time: 14 us; the launch traced here: 13.9 us
  Pallas kernels  12.4 us (89%)
  other arithmetic  0.76 us (5%)
  between operations  0.69 us (5%)
    pallas_call x1, Pallas kernels, body(): pl.pallas_call(functools.partial(kernel, n), out_shape=pltpu.VMEM((rows_h...  12.4 us
    add x1, other arithmetic, body(): updated = iterate + precond[:, None] * residual  0.76 us

profile of v1, /device:TPU:1, one launch (start us, length us, event | category | flops | bytes accessed | tf_op | source)
XLA Modules:
  0.0 13.9 jit_solution(8527650676377378491)
XLA Ops:
  0.6 0.0 copy-start
  0.6 0.0 copy-start.1
  0.7 0.0 copy-start.2
  0.7 12.4 %shard_map.113 = f32[256,128]{1,0:T(8,128)S(1)} custom-call(f32[256,128]{1,0:T(8,128)} %iterate_hbm.1, f32[1,384,384]{2,1,0:T(8,128)} %schur_hbm.1, f32[256,256]{1,0:T(8,128)} %near_hbm.1, f32[16,32,256]{2,1,0:T(8,128)} %u_hbm.1, f32[16,32,256]{2,1,0:T(8,128)} %v_hbm.1, s32[1,16]{1,0:T(1,128)} %bitcast.3, s32[3,1,128]{2,1,0:T(1,128)} %bitcast.2, ...), custom_call_target="tpu_custom_call" | custom-call | tf_op jit(solution)/shard_map/pallas_call | solution.py:388
  13.1 0.0 copy-done
  13.1 0.0 copy-done.1
  13.1 0.0 copy-done.2
  13.1 0.8 %multiply_add_fusion = (f32[256,128]{1,0:T(8,128)}, f32[256,128]{1,0:T(8,128)}) fusion(f32[256,128]{1,0:T(8,128)S(1)} %copy-done, f32[256]{0:T(256)S(1)} %copy-done.2, f32[256,128]{1,0:T(8,128)S(1)} %copy-done.1, f32[256,128]{1,0:T(8,128)S(1)} %shard_map.113), kind=kLoop, calls=%fused_computation | loop fusion | flops 98304 | bytes 656384 | tf_op jit(solution)/shard_map/add | solution.py:420
Async XLA Ops:
  0.6 12.4 %copy-start = (f32[256,128]{1,0:T(8,128)S(1)}, f32[256,128]{1,0:T(8,128)}, u32[]{:S(2)}) copy-start(f32[256,128]{1,0:T(8,128)} %iterate_hbm.1) | copy-start | bytes 393220
  0.6 12.4 %copy-start.1 = (f32[256,128]{1,0:T(8,128)S(1)}, f32[256,128]{1,0:T(8,128)}, u32[]{:S(2)}) copy-start(f32[256,128]{1,0:T(8,128)} %param.11) | copy-start | bytes 393220
  0.7 12.4 %copy-start.2 = (f32[256]{0:T(256)S(1)}, f32[256]{0:T(256)}, u32[]{:S(2)}) copy-start(f32[256]{0:T(256)} %param.19) | copy-start | bytes 3076

commit v2 on v1

--- a/solution.py
+++ b/solution.py
@@ -11,6 +11,15 @@
 MESH = pl.DeviceIdType.MESH
 F32 = jnp.float32
 BF16 = jnp.bfloat16
+
+ALL, NEAR, FAR = 0, 1, 2
+PLANS = [
+    {0: [(0, NEAR)], 1: [(0, ALL)], 2: [(0, ALL)], 3: [(0, ALL)]},
+    {0: [(1, ALL)], 1: [(1, ALL)], 3: [(1, ALL)]},
+    {0: [(2, ALL), (0, FAR)], 3: [(2, ALL), (3, ALL)]},
+    {2: [(1, ALL)]},
+    {0: [(3, ALL)], 1: [(3, ALL), (2, ALL)], 2: [(3, ALL), (2, ALL)]},
+]
 
 
 def halves(x):
@@ -67,7 +76,7 @@
     if blocks == 4:
         send_order = [by_block(1, 2, 0, 0), by_block(0, 0, 1, 1), by_block(2, 1, 2, 2), 3]
         own_slot = by_block(1, 2, 2, 3)
-        recv_order = [block, by_block(1, 0, 1, 2), by_block(2, 2, 0, 1), by_block(3, 3, 3, 0)]
+        recv_order = [block, by_block(1, 0, 1, 2), by_block(3, 2, 0, 1), by_block(2, 3, 3, 0)]
     else:
         send_order, own_slot, recv_order = [0], 0, [0]
 
@@ -182,42 +191,60 @@
             sent[at + g] = jnp.where(rank_ids < rank[0, first + g], part, 0.0)
 
     paired = group & (group - 1) == 0 and group > 1
-    if paired:
-        offsets = [int(bin(group + k)[:2:-1], 2) for k in range(group)]
-        flip = lax.rem(me, 2) * (group // 2)
+    half = group // 2
+
+    def flipped(k):
+        moved = place_in_group
+        for bit in [1 << b for b in range(group.bit_length()) if k >> b & 1]:
+            moved = moved + bit * (1 - 2 * lax.rem(lax.div(place_in_group, bit), 2))
+        return moved
 
     def member(k):
         if not paired:
             return lax.rem(place_in_group + k, group)
-        moved = place_in_group
-        for bit in [1 << b for b in range(group.bit_length() - 1)]:
-            on = 1 if offsets[k] & bit else 0
-            change = on + lax.rem(me, 2) - 2 * on * lax.rem(me, 2) if bit == group // 2 else on
-            moved = moved + change * bit * (1 - 2 * lax.rem(lax.div(place_in_group, bit), 2))
-        return moved
-
-    def send(slot, c):
-        first = send_order[slot] * per_block + c * group
-        for k in range(group):
-            in_group = member(k)
-
-            def start():
-                pltpu.make_async_remote_copy(
-                    src_ref=sent.at[(slot * chunks + c) * group + in_group], dst_ref=gathered.at[me],
-                    send_sem=send_sem.at[0], recv_sem=recv_sem.at[mine],
-                    device_id={"wide": first + in_group}, device_id_type=MESH,
-                ).start()
-
-            if blocks == 4 and (slot == 0 or paired and offsets[k] not in (0, group // 2)):
-                start()
-            else:
-                pl.when(first + in_group != me)(start)
+        k = int(bin(group + k)[:2:-1], 2)
+        core = lax.rem(me, 2)
+        return flipped(k) + core * (flipped(k ^ half) - flipped(k))
+
+    def start(slot, c, in_group, may_be_me):
+        target = send_order[slot] * per_block + c * group + in_group
+
+        def go():
+            pltpu.make_async_remote_copy(
+                src_ref=sent.at[(slot * chunks + c) * group + in_group], dst_ref=gathered.at[me],
+                send_sem=send_sem.at[0], recv_sem=recv_sem.at[mine],
+                device_id={"wide": target}, device_id_type=MESH,
+            ).start()
+
+        if may_be_me:
+            pl.when(target != me)(go)
+        else:
+            go()
+
+    def send(stage):
+        if blocks == 1:
+            if stage == 2:
+                for c in range(chunks):
+                    for k in range(group):
+                        start(0, c, member(k), True)
+            return
+        for b, plan in PLANS[stage].items():
+            @pl.when(block == b)
+            def _():
+                for slot, part in plan:
+                    own = slot == [1, 2, 2, 3][b]
+                    for c in range(chunks):
+                        if part == ALL or not paired:
+                            if part == FAR:
+                                continue
+                            for k in range(group):
+                                start(slot, c, member(k), own)
+                        else:
+                            for k in range(half) if part == NEAR else range(half, group):
+                                start(slot, c, flipped(k), own and (k == 0 or chunks > 1))
 
     rank_load.wait()
     steps = [(slot, c) for slot in range(blocks) for c in range(chunks)]
-
-    def of_slot(slot):
-        return [(slot, c) for c in range(chunks)]
 
     compress(*steps[0])
     enter()
@@ -232,17 +259,17 @@
     def _():
         face_up.start()
 
-    send(*steps[0])
-    for step in steps[1 : 2 * chunks]:
+    for step in steps[1:chunks]:
         compress(*step)
-        send(*step)
+    send(0)
+    for step in steps[chunks : 2 * chunks]:
+        compress(*step)
+    send(1)
     for step in steps[2 * chunks :]:
         compress(*step)
     gathered[me] = sent[own_slot * per_block + place_in_block]
-    if blocks == 4:
-        late(0)
-        for step in of_slot(2):
-            send(*step)
+    late(0)
+    send(2)
 
     in_face[1] = picked(1)
     near_load.wait()
@@ -254,6 +281,7 @@
         u_high[at] = high
         u_low[at] = low
 
+    send(3)
     schur_load.wait()
     s_high, s_low = halves(schur[0])
 
@@ -263,15 +291,13 @@
         return product(s_high[:, span], s_low[:, span], b_both, b_high)
 
     force = force_part(1)
-    if blocks == 4:
-        late(1)
-
-        @pl.when(waits_above)
-        def _():
-            face_up.start()
-
-        for step in of_slot(3):
-            send(*step)
+    late(1)
+
+    @pl.when(waits_above)
+    def _():
+        face_up.start()
+
+    send(4)
 
     def face_wait():
         @pl.when(has_above)
@@ -303,7 +329,7 @@
         b_both, _ = pair(in_force[o])
         return fold(mm(scatter, b_both))
 
-    def far(slot, c):
+    def far_wait(slot, c):
         at = recv_order[slot] * chunks + c
 
         def arrived(tiles):
@@ -328,14 +354,18 @@
                     arrived(group)
 
         wait()
+
+    def far(slot, c):
+        at = recv_order[slot] * chunks + c
         got = gathered[pl.ds(at * group, group)].reshape(group * rank_top, loads)
         b_both, b_high = pair(got)
         return product(u_high[at], u_low[at], b_both, b_high)
 
     out_ref[...] += scattered(1)
     order = [(slot, c) for slot in range(blocks) for c in range(chunks)]
-    for slot, c in order[:-1]:
-        out_ref[...] += far(slot, c)
+    for step in order[:-1]:
+        far_wait(*step)
+        out_ref[...] += far(*step)
 
     def force_wait():
         @pl.when(has_below)
@@ -346,9 +376,9 @@
         def _():
             force_down.wait_recv()
 
+    far_wait(*order[-1])
     force_wait()
-    out_ref[...] += scattered(0) + scattered(2)
-    out_ref[...] += far(*order[-1])
+    out_ref[...] += far(*order[-1]) + (scattered(0) + scattered(2))
 
     def sent_wait():
         @pl.when(has_below)

time: 14 us -> 13.5 us (0.964)
  Pallas kernels: 12.4 us -> 11.9 us
    pallas_call x1, Pallas kernels: 12.4 us -> 11.9 us  [body(): pl.pallas_call(functools.partial(kernel, n), out_shape=pltpu.VMEM((rows_h...]
where the time goes in v2:
time: 13.5 us; the launch traced here: 13.4 us
  Pallas kernels  11.9 us (88%)
  other arithmetic  0.76 us (6%)
  between operations  0.69 us (5%)
    pallas_call x1, Pallas kernels, body(): pl.pallas_call(functools.partial(kernel, n), out_shape=pltpu.VMEM((rows_h...  11.9 us
    add x1, other arithmetic, body(): updated = iterate + precond[:, None] * residual  0.76 us

profile of v2, /device:TPU:1, one launch (start us, length us, event | category | flops | bytes accessed | tf_op | source)
XLA Modules:
  0.0 13.4 jit_solution(9926365904547522650)
XLA Ops:
  0.6 0.0 copy-start
  0.6 0.0 copy-start.1
  0.7 0.0 copy-start.2
  0.7 11.9 %shard_map.113 = f32[256,128]{1,0:T(8,128)S(1)} custom-call(f32[256,128]{1,0:T(8,128)} %iterate_hbm.1, f32[1,384,384]{2,1,0:T(8,128)} %schur_hbm.1, f32[256,256]{1,0:T(8,128)} %near_hbm.1, f32[16,32,256]{2,1,0:T(8,128)} %u_hbm.1, f32[16,32,256]{2,1,0:T(8,128)} %v_hbm.1, s32[1,16]{1,0:T(1,128)} %bitcast.3, s32[3,1,128]{2,1,0:T(1,128)} %bitcast.2, ...), custom_call_target="tpu_custom_call" | custom-call | tf_op jit(solution)/shard_map/pallas_call | solution.py:418
  12.6 0.0 copy-done
  12.6 0.0 copy-done.1
  12.6 0.0 copy-done.2
  12.6 0.8 %multiply_add_fusion = (f32[256,128]{1,0:T(8,128)}, f32[256,128]{1,0:T(8,128)}) fusion(f32[256,128]{1,0:T(8,128)S(1)} %copy-done, f32[256]{0:T(256)S(1)} %copy-done.2, f32[256,128]{1,0:T(8,128)S(1)} %copy-done.1, f32[256,128]{1,0:T(8,128)S(1)} %shard_map.113), kind=kLoop, calls=%fused_computation | loop fusion | flops 98304 | bytes 656384 | tf_op jit(solution)/shard_map/add | solution.py:450
Async XLA Ops:
  0.6 12.0 %copy-start = (f32[256,128]{1,0:T(8,128)S(1)}, f32[256,128]{1,0:T(8,128)}, u32[]{:S(2)}) copy-start(f32[256,128]{1,0:T(8,128)} %iterate_hbm.1) | copy-start | bytes 393220
  0.6 12.0 %copy-start.1 = (f32[256,128]{1,0:T(8,128)S(1)}, f32[256,128]{1,0:T(8,128)}, u32[]{:S(2)}) copy-start(f32[256,128]{1,0:T(8,128)} %param.11) | copy-start | bytes 393220
  0.7 12.0 %copy-start.2 = (f32[256]{0:T(256)S(1)}, f32[256]{0:T(256)}, u32[]{:S(2)}) copy-start(f32[256]{0:T(256)} %param.19) | copy-start | bytes 3076

commit v3 on v2

--- a/solution.py
+++ b/solution.py
@@ -13,12 +13,14 @@
 BF16 = jnp.bfloat16
 
 ALL, NEAR, FAR = 0, 1, 2
+EACH, FIRST, REST, LOW, HIGH = range(5)
 PLANS = [
-    {0: [(0, NEAR)], 1: [(0, ALL)], 2: [(0, ALL)], 3: [(0, ALL)]},
-    {0: [(1, ALL)], 1: [(1, ALL)], 3: [(1, ALL)]},
-    {0: [(2, ALL), (0, FAR)], 3: [(2, ALL), (3, ALL)]},
-    {2: [(1, ALL)]},
-    {0: [(3, ALL)], 1: [(3, ALL), (2, ALL)], 2: [(3, ALL), (2, ALL)]},
+    {0: [(0, NEAR, EACH)], 1: [(0, ALL, FIRST), (0, ALL, REST)], 2: [(0, ALL, EACH)], 3: [(0, ALL, EACH)]},
+    {0: [(1, ALL, EACH)], 1: [(1, ALL, REST)]},
+    {0: [(2, ALL, EACH), (0, FAR, EACH)], 1: [(1, ALL, FIRST)], 3: [(2, ALL, EACH), (3, ALL, EACH)]},
+    {2: [(1, ALL, EACH)], 3: [(1, ALL, EACH)]},
+    {0: [(3, ALL, EACH)], 1: [(3, ALL, LOW), (3, FAR, HIGH), (2, ALL, EACH)], 2: [(3, ALL, EACH), (2, ALL, EACH)]},
+    {1: [(3, NEAR, HIGH)]},
 ]
 
 
@@ -74,7 +76,8 @@
         return first + (second - first) * at_least[0] + (third - second) * at_least[1] + (fourth - third) * at_least[2]
 
     if blocks == 4:
-        send_order = [by_block(1, 2, 0, 0), by_block(0, 0, 1, 1), by_block(2, 1, 2, 2), 3]
+        upper = lax.div(place_in_block + per_block - 1, per_block)
+        send_order = [by_block(1, 2 * upper, 0, 0), by_block(0, 2 - 2 * upper, 1, 1), by_block(2, 1, 2, 2), 3]
         own_slot = by_block(1, 2, 2, 3)
         recv_order = [block, by_block(1, 0, 1, 2), by_block(3, 2, 0, 1), by_block(2, 3, 3, 0)]
     else:
@@ -90,7 +93,13 @@
         at = slot * chunks + c
         return load(7 + at, v_hbm.at[pl.ds(first, group)], v.at[pl.ds(at * group, group)])
 
-    iterate_load = load(0, iterate_hbm, iterate)
+    rows_load = load(2, rows_hbm, rows)
+    count_load = load(3, count_hbm, count)
+    quarter = rows_here // 4
+    for part in range(4):
+        span = pl.ds(part * quarter, quarter)
+        pltpu.make_async_copy(iterate_hbm.at[span], iterate.at[span], load_sem.at[0]).start()
+    iterate_load = pltpu.make_async_copy(iterate_hbm, iterate, load_sem.at[0])
     barrier = pltpu.get_barrier_semaphore()
 
     def tell(semaphore, target):
@@ -99,25 +108,35 @@
     def tell_block(semaphore, target_block):
         for k in range(per_block):
             tell(semaphore, target_block * per_block + lax.rem(place_in_block + k, per_block))
+
+    def tell_rest(semaphore, target_block):
+        rest = per_block - 1
+        for k in range(rest):
+            tell(semaphore, target_block * per_block + 1 + lax.rem(place_in_block + k, rest))
 
     for k in range(1, per_block):
         tell(barrier, block * per_block + lax.rem(place_in_block + k, per_block))
     if blocks == 4:
         for target in range(blocks):
-            last = [1, 2, 2, 3][target]
+            last = [1, 1, 2, 3][target]
 
             @pl.when(jnp.logical_and(block != target, block <= last))
             def _():
                 tell_block(barrier, target)
 
+        @pl.when(block == 2)
+        def _():
+            tell_rest(barrier, 1)
+
     def enter():
-        pl.semaphore_wait(barrier, (per_block * by_block(2, 3, 3, 4) if blocks == 4 else n) - 1)
+        pl.semaphore_wait(barrier, (per_block * by_block(2, 2 + upper, 3, 4) if blocks == 4 else n) - 1)
 
     def announce():
         if blocks == 4:
             @pl.when(block == 2)
             def _():
                 tell_block(late_sem.at[0], 0)
+                tell(late_sem.at[0], per_block)
 
             @pl.when(block == 3)
             def _():
@@ -126,12 +145,10 @@
 
     def late(which):
         if blocks == 4:
-            @pl.when(block == 0 if which == 0 else block < 3)
+            @pl.when(me < per_block + 1 if which == 0 else block < 3)
             def _():
                 pl.semaphore_wait(late_sem.at[which], per_block)
 
-    rows_load = load(2, rows_hbm, rows)
-    count_load = load(3, count_hbm, count)
     rank_load = load(1, rank_hbm, rank)
     v_loads = {(slot, c): load_v(slot, c) for slot in range(blocks) for c in range(chunks)}
     near_load = load(6, near_hbm, near)
@@ -162,17 +179,22 @@
     force_up = edge_copy(1, 1, in_force.at[0], force_recv.at[0])
     force_down = edge_copy(0, 1, in_force.at[2], force_recv.at[1])
 
-    iterate_load.wait()
-    it_both, it_high = pair(iterate[...])
     rows_load.wait()
     count_load.wait()
     slot_ids = lax.broadcasted_iota(jnp.int32, (1, face), 1)
     row_of = [jnp.where(slot_ids < count[0, o], rows[o], -1) for o in range(3)]
     lanes = lax.broadcasted_iota(jnp.int32, (face, rows_here), 1)
 
+    def selection(o):
+        column = jnp.broadcast_to(row_of[o].astype(F32), (face, face)).T[:, :1].astype(jnp.int32)
+        return (column == lanes).astype(F32).astype(BF16)
+
+    selections = [selection(0), None, selection(2)]
+    iterate_load.wait()
+    it_both, it_high = pair(iterate[...])
+
     def picked(o):
-        column = jnp.broadcast_to(row_of[o].astype(F32), (face, face)).T[:, :1].astype(jnp.int32)
-        select = (column == lanes).astype(F32).astype(BF16)
+        select = selection(o) if selections[o] is None else selections[o]
         return fold(mm(select, it_both))
 
     edge_out[0, 0] = picked(0)
@@ -220,6 +242,18 @@
             pl.when(target != me)(go)
         else:
             go()
+
+    def send_slot(b, slot, part):
+        own = slot == [1, 2, 2, 3][b]
+        for c in range(chunks):
+            if part == ALL or not paired:
+                if part == FAR:
+                    continue
+                for k in range(group):
+                    start(slot, c, member(k), own)
+            else:
+                for k in range(half) if part == NEAR else range(half, group):
+                    start(slot, c, flipped(k), own and (k == 0 or chunks > 1))
 
     def send(stage):
         if blocks == 1:
@@ -231,17 +265,13 @@
         for b, plan in PLANS[stage].items():
             @pl.when(block == b)
             def _():
-                for slot, part in plan:
-                    own = slot == [1, 2, 2, 3][b]
-                    for c in range(chunks):
-                        if part == ALL or not paired:
-                            if part == FAR:
-                                continue
-                            for k in range(group):
-                                start(slot, c, member(k), own)
-                        else:
-                            for k in range(half) if part == NEAR else range(half, group):
-                                start(slot, c, flipped(k), own and (k == 0 or chunks > 1))
+                for slot, part, who in plan:
+                    if who == EACH:
+                        send_slot(b, slot, part)
+                    else:
+                        high = lax.div(place_in_block, per_block // 2)
+                        chosen = {FIRST: upper == 0, REST: upper == 1, LOW: high == 0, HIGH: high == 1}[who]
+                        pl.when(chosen)(functools.partial(send_slot, b, slot, part))
 
     rank_load.wait()
     steps = [(slot, c) for slot in range(blocks) for c in range(chunks)]
@@ -322,6 +352,7 @@
     def _():
         force_down.start()
 
+    send(5)
     place = lax.broadcasted_iota(jnp.int32, (rows_here, face), 0)
 
     def scattered(o):

time: 13.5 us -> 13.3 us (0.985)
  the two profiles are of different devices: /device:TPU:1 before, /device:TPU:9 now
where the time goes in v3:
time: 13.3 us; the launch traced here: 13.1 us
  Pallas kernels  11.7 us (88%)
  other arithmetic  0.76 us (6%)
  between operations  0.69 us (5%)
    pallas_call x1, Pallas kernels, body(): pl.pallas_call(functools.partial(kernel, n), out_shape=pltpu.VMEM((rows_h...  11.7 us
    add x1, other arithmetic, body(): updated = iterate + precond[:, None] * residual  0.76 us

profile of v3, /device:TPU:9, one launch (start us, length us, event | category | flops | bytes accessed | tf_op | source)
XLA Modules:
  0.0 13.1 jit_solution(6483509666170414273)
XLA Ops:
  0.6 0.0 copy-start
  0.6 0.0 copy-start.1
  0.7 0.0 copy-start.2
  0.7 11.7 %shard_map.113 = f32[256,128]{1,0:T(8,128)S(1)} custom-call(f32[256,128]{1,0:T(8,128)} %iterate_hbm.1, f32[1,384,384]{2,1,0:T(8,128)} %schur_hbm.1, f32[256,256]{1,0:T(8,128)} %near_hbm.1, f32[16,32,256]{2,1,0:T(8,128)} %u_hbm.1, f32[16,32,256]{2,1,0:T(8,128)} %v_hbm.1, s32[1,16]{1,0:T(1,128)} %bitcast.3, s32[3,1,128]{2,1,0:T(1,128)} %bitcast.2, ...), custom_call_target="tpu_custom_call" | custom-call | tf_op jit(solution)/shard_map/pallas_call | solution.py:449
  12.4 0.0 copy-done
  12.4 0.0 copy-done.1
  12.4 0.0 copy-done.2
  12.4 0.8 %multiply_add_fusion = (f32[256,128]{1,0:T(8,128)}, f32[256,128]{1,0:T(8,128)}) fusion(f32[256,128]{1,0:T(8,128)S(1)} %copy-done, f32[256]{0:T(256)S(1)} %copy-done.2, f32[256,128]{1,0:T(8,128)S(1)} %copy-done.1, f32[256,128]{1,0:T(8,128)S(1)} %shard_map.113), kind=kLoop, calls=%fused_computation | loop fusion | flops 98304 | bytes 656384 | tf_op jit(solution)/shard_map/add | solution.py:481
Async XLA Ops:
  0.6 11.7 %copy-start = (f32[256,128]{1,0:T(8,128)S(1)}, f32[256,128]{1,0:T(8,128)}, u32[]{:S(2)}) copy-start(f32[256,128]{1,0:T(8,128)} %iterate_hbm.1) | copy-start | bytes 393220
  0.6 11.7 %copy-start.1 = (f32[256,128]{1,0:T(8,128)S(1)}, f32[256,128]{1,0:T(8,128)}, u32[]{:S(2)}) copy-start(f32[256,128]{1,0:T(8,128)} %param.11) | copy-start | bytes 393220
  0.7 11.7 %copy-start.2 = (f32[256]{0:T(256)S(1)}, f32[256]{0:T(256)}, u32[]{:S(2)}) copy-start(f32[256]{0:T(256)} %param.19) | copy-start | bytes 3076

commit v4 on v3

--- a/solution.py
+++ b/solution.py
@@ -18,8 +18,8 @@
     {0: [(0, NEAR, EACH)], 1: [(0, ALL, FIRST), (0, ALL, REST)], 2: [(0, ALL, EACH)], 3: [(0, ALL, EACH)]},
     {0: [(1, ALL, EACH)], 1: [(1, ALL, REST)]},
     {0: [(2, ALL, EACH), (0, FAR, EACH)], 1: [(1, ALL, FIRST)], 3: [(2, ALL, EACH), (3, ALL, EACH)]},
-    {2: [(1, ALL, EACH)], 3: [(1, ALL, EACH)]},
-    {0: [(3, ALL, EACH)], 1: [(3, ALL, LOW), (3, FAR, HIGH), (2, ALL, EACH)], 2: [(3, ALL, EACH), (2, ALL, EACH)]},
+    {1: [(2, ALL, HIGH)], 2: [(1, ALL, EACH)], 3: [(1, ALL, EACH)]},
+    {0: [(3, ALL, EACH)], 1: [(3, ALL, LOW), (3, FAR, HIGH), (2, ALL, LOW)], 2: [(3, ALL, EACH), (2, ALL, EACH)]},
     {1: [(3, NEAR, HIGH)]},
 ]
 
@@ -91,10 +91,10 @@
     def load_v(slot, c):
         first = send_order[slot] * per_block + c * group
         at = slot * chunks + c
-        return load(7 + at, v_hbm.at[pl.ds(first, group)], v.at[pl.ds(at * group, group)])
-
-    rows_load = load(2, rows_hbm, rows)
-    count_load = load(3, count_hbm, count)
+        return load(3 + at, v_hbm.at[pl.ds(first, group)], v.at[pl.ds(at * group, group)])
+
+    rows_load = load(1, rows_hbm, rows)
+    count_load = load(1, count_hbm, count)
     quarter = rows_here // 4
     for part in range(4):
         span = pl.ds(part * quarter, quarter)
@@ -151,9 +151,9 @@
 
     rank_load = load(1, rank_hbm, rank)
     v_loads = {(slot, c): load_v(slot, c) for slot in range(blocks) for c in range(chunks)}
-    near_load = load(6, near_hbm, near)
-    u_load = load(5, u_hbm, u)
-    schur_load = load(4, schur_hbm, schur)
+    near_load = load(2, near_hbm, near)
+    u_load = load(2, u_hbm, u)
+    schur_load = load(2, schur_hbm, schur)
 
     @pl.when(me == 0)
     def _():
@@ -181,6 +181,7 @@
 
     rows_load.wait()
     count_load.wait()
+    rank_load.wait()
     slot_ids = lax.broadcasted_iota(jnp.int32, (1, face), 1)
     row_of = [jnp.where(slot_ids < count[0, o], rows[o], -1) for o in range(3)]
     lanes = lax.broadcasted_iota(jnp.int32, (face, rows_here), 1)
@@ -273,7 +274,6 @@
                         chosen = {FIRST: upper == 0, REST: upper == 1, LOW: high == 0, HIGH: high == 1}[who]
                         pl.when(chosen)(functools.partial(send_slot, b, slot, part))
 
-    rank_load.wait()
     steps = [(slot, c) for slot in range(blocks) for c in range(chunks)]
 
     compress(*steps[0])
@@ -303,16 +303,16 @@
 
     in_face[1] = picked(1)
     near_load.wait()
+    u_load.wait()
+    schur_load.wait()
     near_high, near_low = halves(near[...])
     out_ref[...] = product(near_high, near_low, it_both, it_high)
-    u_load.wait()
     for at in range(n // group):
         high, low = halves(u[at * group : (at + 1) * group].reshape(group * rank_top, rows_here).T)
         u_high[at] = high
         u_low[at] = low
 
     send(3)
-    schur_load.wait()
     s_high, s_low = halves(schur[0])
 
     def force_part(o):
@@ -467,7 +467,7 @@
             pltpu.VMEM((n, rank_top, loads), F32),
             pltpu.VMEM((n // group, rows_here, group * rank_top), BF16),
             pltpu.VMEM((n // group, rows_here, group * rank_top), BF16),
-            dma((7 + n // group,)),
+            dma((3 + n // group,)),
             dma((2,)),
             dma((2,)),
             dma((2,)),

time: 13.3 us -> 13.3 us (level)
  the two profiles are of different devices: /device:TPU:9 before, /device:TPU:25 now
where the time goes in v4:
time: 13.3 us; the launch traced here: 13.2 us
  Pallas kernels  11.7 us (88%)
  other arithmetic  0.76 us (6%)
  between operations  0.69 us (5%)
    pallas_call x1, Pallas kernels, body(): pl.pallas_call(functools.partial(kernel, n), out_shape=pltpu.VMEM((rows_h...  11.7 us
    add x1, other arithmetic, body(): updated = iterate + precond[:, None] * residual  0.76 us

profile of v4, /device:TPU:25, one launch (start us, length us, event | category | flops | bytes accessed | tf_op | source)
XLA Modules:
  0.0 13.2 jit_solution(7710605277099757589)
XLA Ops:
  0.6 0.0 copy-start
  0.6 0.0 copy-start.1
  0.7 0.0 copy-start.2
  0.7 11.7 %shard_map.113 = f32[256,128]{1,0:T(8,128)S(1)} custom-call(f32[256,128]{1,0:T(8,128)} %iterate_hbm.1, f32[1,384,384]{2,1,0:T(8,128)} %schur_hbm.1, f32[256,256]{1,0:T(8,128)} %near_hbm.1, f32[16,32,256]{2,1,0:T(8,128)} %u_hbm.1, f32[16,32,256]{2,1,0:T(8,128)} %v_hbm.1, s32[1,16]{1,0:T(1,128)} %bitcast.3, s32[3,1,128]{2,1,0:T(1,128)} %bitcast.2, ...), custom_call_target="tpu_custom_call" | custom-call | tf_op jit(solution)/shard_map/pallas_call | solution.py:449
  12.4 0.0 copy-done
  12.4 0.0 copy-done.1
  12.4 0.0 copy-done.2
  12.4 0.8 %multiply_add_fusion = (f32[256,128]{1,0:T(8,128)}, f32[256,128]{1,0:T(8,128)}) fusion(f32[256,128]{1,0:T(8,128)S(1)} %copy-done, f32[256]{0:T(256)S(1)} %copy-done.2, f32[256,128]{1,0:T(8,128)S(1)} %copy-done.1, f32[256,128]{1,0:T(8,128)S(1)} %shard_map.113), kind=kLoop, calls=%fused_computation | loop fusion | flops 98304 | bytes 656384 | tf_op jit(solution)/shard_map/add | solution.py:481
Async XLA Ops:
  0.6 11.7 %copy-start = (f32[256,128]{1,0:T(8,128)S(1)}, f32[256,128]{1,0:T(8,128)}, u32[]{:S(2)}) copy-start(f32[256,128]{1,0:T(8,128)} %iterate_hbm.1) | copy-start | bytes 393220
  0.6 11.7 %copy-start.1 = (f32[256,128]{1,0:T(8,128)S(1)}, f32[256,128]{1,0:T(8,128)}, u32[]{:S(2)}) copy-start(f32[256,128]{1,0:T(8,128)} %param.11) | copy-start | bytes 393220
  0.7 11.7 %copy-start.2 = (f32[256]{0:T(256)S(1)}, f32[256]{0:T(256)}, u32[]{:S(2)}) copy-start(f32[256]{0:T(256)} %param.19) | copy-start | bytes 3076
